TPU v7x, 256 devices: a whole 4x4x8 slice. The times are simulated.
256 devices in a mesh: ax: 64 (over y_lo, z, x), sec: 4 (over y_hi, core).
Axes of the slice: x: 4, y: 4 (y_hi: 2, y_lo: 2; y = y_hi * 2 + y_lo), z: 8, core: 2. Of those that a mesh axis runs over, the one named last changes fastest.
Arguments:
- load: float32 [8192, 6, 1024], P('ax', None, 'sec'), may hold values from -6 to 6
- disp: float32 [8192, 6, 1024], P('ax', None, 'sec'), may hold values from -1.5 to 1.5
- stiff: float32 [8192, 6, 1024], P('ax', None, 'sec'), may hold values from 0.5 to 2
- hole: int32 [8192, 1024], P('ax', 'sec'), may hold values 0 or 1
- section_class: int32 [8192], P('ax'), may hold values from 0 to 3
- class_table: float32 [4, 6], replicated, may hold values from 0.5 to 2
- precond: float32 [6, 6, 1024], replicated, may hold values from -0.5 to 0.5, as said below
Outputs:
- disp_new: float32 [8192, 6, 1024], P('ax', None, 'sec')
- residual_new: float32 [8192, 6, 1024], P('ax', None, 'sec')
- stats: float32 [3], replicated
Inputs may be any that keep to these rules, and one draw needn't show every extreme that they name: `precond`: for each harmonic the matrix over the first two dimensions is symmetric and positive definite.
All inputs are finite; a program needn't handle non-finite values. No bound on the sum of `hole` on one device may be relied on, other than what follows from the above.
Results may differ from a plain program's by a relative error of at most 0.0075.
Values sent between devices are 32-bit elements; how exact they have to be, the bound alone decides.
A program may use at most 64 MiB of HBM per device.

v0:
```python
import math
import jax
import jax.numpy as jnp
from jax import lax
from jax.sharding import PartitionSpec as P


def with_halo(x, sides, width, wrap):
    for axis, dim in sides:
        size, length = (lax.axis_size(axis), x.shape[dim])
        up = [(i, (i + 1) % size) for i in range(size if wrap else size - 1)]
        down = [(j, i) for i, j in up]
        last = lax.slice_in_dim(x, length - width, length, axis=dim)
        first = lax.slice_in_dim(x, 0, width, axis=dim)
        before = lax.ppermute(last, axis, up)
        after = lax.ppermute(first, axis, down)
        x = jnp.concatenate([before, x, after], axis=dim)
    return x


def swap_radial(field):
    extent = field.shape
    folded = field.reshape(extent[0], extent[1] // 2, 2, extent[2])
    return jnp.flip(folded, axis=2).reshape(extent)


def apply_operator(field, stiffness):
    axial_pad = with_halo(field, (("ax", 0),), 1, False)
    sector_pad = with_halo(field, (("sec", 2),), 1, True)
    beside = axial_pad[2:] + axial_pad[:-2]
    beside = beside + sector_pad[:, :, 2:] + sector_pad[:, :, :-2]
    return (stiffness + 4.5) * field - beside - 0.5 * swap_radial(field)


def harmonic_table(row_index, col_index, length):
    product = row_index[:, None] * col_index[None, :] % length
    angle = 2.0 * math.pi / length * product.astype(jnp.float32)
    return jnp.concatenate([jnp.cos(angle), jnp.sin(angle)], axis=1)


def scale_harmonics(block_inverse, spectrum):
    doubled = jnp.concatenate([block_inverse, block_inverse], axis=2)
    return jnp.sum(doubled[None] * spectrum[:, None], axis=2)


def shards(load, disp, stiff, hole, section_class, class_table, precond):
    slab_count, comp_count, sector_width = disp.shape
    sector_count = lax.axis_size("sec")
    around_cells = sector_width * sector_count
    total_axial = slab_count * lax.axis_size("ax")
    position = lax.axis_index("ax") * slab_count + jnp.arange(slab_count)
    taper = 1.0 + 2.0 * position.astype(jnp.float32) / (total_axial - 1)
    one_hot = (section_class[:, None] == jnp.arange(class_table.shape[0])[None, :]).astype(
        jnp.float32
    )
    factors = jnp.dot(one_hot, class_table, precision=lax.Precision.HIGHEST)
    stiffness = stiff * (factors * taper[:, None])[:, :, None]
    solid = (1 - hole).astype(jnp.float32)[:, None, :]
    residual = solid * (load - apply_operator(disp, stiffness))
    sector = lax.axis_index("sec")
    own_index = sector * sector_width + jnp.arange(sector_width)
    table = harmonic_table(jnp.arange(around_cells), own_index, around_cells)
    own_inverse = lax.dynamic_slice_in_dim(precond, sector * sector_width, sector_width, 2)
    initial = jnp.zeros((slab_count, comp_count, 2 * sector_width), jnp.float32)
    piece = lax.all_gather(residual, "sec", axis=2, tiled=True)
    span = piece.shape[2]
    table_rows = table
    flat = piece.reshape(-1, span)
    spectrum = jnp.dot(flat, table_rows, precision=lax.Precision.HIGHEST).reshape(initial.shape)
    scaled = scale_harmonics(own_inverse, spectrum).reshape(-1, 2 * sector_width)
    table_rows = table
    shares = lax.psum_scatter(
        lax.dot_general(
            table_rows, scaled, (((1,), (1,)), ((), ())), precision=lax.Precision.HIGHEST
        )
        / around_cells,
        "sec",
        scatter_dimension=0,
        tiled=True,
    )
    smoothed = shares.T.reshape(slab_count, comp_count, sector_width)
    prec = solid * smoothed
    image = solid * apply_operator(prec, stiffness)
    cell_total = slab_count * lax.axis_size("ax") * comp_count * around_cells
    inner_rz = lax.psum(jnp.sum(residual * prec), ("ax", "sec")) / cell_total
    inner_zq = lax.psum(jnp.sum(prec * image), ("ax", "sec")) / cell_total
    alpha = inner_rz / inner_zq
    residual_new = residual - alpha * image
    square_new = lax.psum(jnp.sum(residual_new * residual_new), ("ax", "sec")) / cell_total
    disp_new = disp + alpha * prec
    return (disp_new, residual_new, jnp.stack([inner_rz, inner_zq, square_new]))


def solution(mesh):
    in_specs = (
        P("ax", None, "sec"),
        P("ax", None, "sec"),
        P("ax", None, "sec"),
        P("ax", "sec"),
        P("ax"),
        P(),
        P(),
    )
    out_specs = (P("ax", None, "sec"), P("ax", None, "sec"), P())
    return jax.shard_map(shards, mesh=mesh, in_specs=in_specs, out_specs=out_specs, check_vma=False)
```

profile of v0, /device:TPU:1, one launch (start us, length us, event | category | flops | bytes accessed | tf_op | source)
XLA Modules:
  0.0 319.1 jit_solution(832956261714137729)
XLA Ops:
  7.3 2.3 fusion.30
  9.5 3.2 %collective-permute-start.2 = (f32[128,6,1]{2,0,1:T(8,128)}, f32[128,6,1]{2,0,1:T(8,128)S(1)}, u32[]{:S(2)}, u32[]{:S(2)}) collective-permute-start(f32[128,6,1]{2,0,1:T(8,128)} %get-tuple-element.16), channel_id=1, source_target_pairs={{1,0},{2,1},{3,2},{0,3},{5,4},{6,5},{7,6},{4,7},{9,8},{10,9},{11,1... | collective-permute-start | bytes 9224 | tf_op jit(solution)/shard_map/ppermute | solution.py:16
  12.8 1.1 collective-permute-start.3
  13.8 0.8 fusion.29
  14.7 1.3 collective-permute-start
  16.0 4.0 %collective-permute-start.1 = (f32[1,6,256]{2,0,1:T(1,128)S(1)}, f32[1,6,256]{2,0,1:T(1,128)S(1)}, u32[]{:S(2)}, u32[]{:S(2)}) collective-permute-start(f32[1,6,256]{2,0,1:T(1,128)S(1)} %get-tuple-element.15), channel_id=1, source_target_pairs={{0,4},{4,8},{8,12},{12,16},{16,20},{20,24},{24,28},{28,32},{32,36}... | collective-permute-start | bytes 18440 | tf_op jit(solution)/shard_map/ppermute | solution.py:15
  20.0 0.9 subtract_convert_fusion
  20.9 0.9 convolution_multiply_fusion.1
  22.0 1.1 collective-permute-done.3
  23.1 1.6 fusion.18
  25.0 4.1 %fusion.22 = (f32[1024,256]{1,0:T(8,128)S(1)}, f32[1024,256]{1,0:T(8,128)S(1)}) fusion(s32[256]{0:T(256)S(1)} %iota_add_fusion), kind=kLoop, calls=%fused_computation.47 | loop fusion | flops 3670016 | bytes 2098176 | tf_op jit(solution)/shard_map/cos | solution.py:38
  29.1 35.1 %all-gather.2.cloned.1.call-done = f32[128,6,1024]{2,0,1:T(8,128)} async-done(((f32[128,6,256]{2,0,1:T(8,128)}), f32[128,6,1024]{2,0,1:T(8,128)}) %all-gather.2.cloned.1.call-update) | async-done | bytes 3145744 | tf_op jit(solution)/shard_map/all_gather | solution.py:65
  64.1 7.0 %fusion = f32[128,6,512]{2,0,1:T(8,128)S(1)} fusion(f32[128,6,1024]{2,0,1:T(8,128)} %all-gather.2.cloned.1.call-done, f32[1024,256]{1,0:T(8,128)S(1)} %get-tuple-element.19, f32[1024,256]{1,0:T(8,128)S(1)} %get-tuple-element.18), kind=kOutput, calls=%fused_computation.2 | convolution fusion | flops 4832362496 | bytes 6815744 | tf_op jit(solution)/shard_map/dot_general | solution.py:69
  71.1 0.7 multiply_reduce_fusion
  71.8 2.3 copy.24
  74.1 2.6 reshape.48
  76.6 8.3 %convolution_multiply_fusion = f32[1024,768]{1,0:T(8,128)} fusion(f32[768,512]{1,0:T(8,128)} %reshape.48, f32[1024,256]{1,0:T(8,128)S(1)} %get-tuple-element.19, f32[1024,256]{1,0:T(8,128)S(1)} %get-tuple-element.18), kind=kOutput, calls=%fused_computation.4 | convolution fusion | flops 4833148928 | bytes 6815744 | tf_op jit(solution)/shard_map/dot_general | solution.py:73
  84.9 49.2 %reduce-scatter.2.cloned.1.call-done = f32[256,768]{1,0:T(8,128)} async-done(((f32[1024,768]{1,0:T(8,128)}), f32[256,768]{1,0:T(8,128)}) %reduce-scatter.2.cloned.1.call-update) | async-done | bytes 786448 | tf_op jit(solution)/shard_map/reduce_scatter | solution.py:72
  134.1 1.4 copy.25
  135.9 1.0 fusion.28
  137.0 2.6 reshape.50
  139.6 0.7 collective-permute-start.6
  140.3 2.6 collective-permute-start.7
  142.8 1.3 collective-permute-start.4
  144.1 4.0 %collective-permute-start.5 = (f32[1,6,256]{2,0,1:T(1,128)S(1)}, f32[1,6,256]{2,0,1:T(1,128)S(1)}, u32[]{:S(2)}, u32[]{:S(2)}) collective-permute-start(f32[1,6,256]{2,0,1:T(1,128)S(1)} %get-tuple-element.11), channel_id=1, source_target_pairs={{0,4},{4,8},{8,12},{12,16},{16,20},{20,24},{24,28},{28,32},{32,36}... | collective-permute-start | bytes 18440 | tf_op jit(solution)/shard_map/ppermute | solution.py:15
  148.1 1.2 copy_multiply_fusion
  149.4 3.3 %collective-permute-done.6 = f32[128,6,1]{2,0,1:T(8,128)S(1)} collective-permute-done((f32[128,6,1]{2,0,1:T(8,128)}, f32[128,6,1]{2,0,1:T(8,128)S(1)}, u32[]{:S(2)}, u32[]{:S(2)}) %collective-permute-start.6) | collective-permute-done | bytes 3104 | tf_op jit(solution)/shard_map/ppermute | solution.py:16
  152.8 2.2 multiply_reduce_fusion.2
  154.9 77.7 %all-reduce = (f32[]{:T(128)}, f32[]{:T(128)}) all-reduce(f32[]{:T(128)} %get-tuple-element.4, f32[]{:T(128)} %get-tuple-element.3), channel_id=1, replica_groups=mesh['ax'=64,'sec'=4] {'ax','sec'}, use_global_device_ids=true, to_apply=%region_3.4 | all-reduce | flops 2 | bytes 16 | tf_op jit(solution)/shard_map/psum | solution.py:85
  234.0 1.2 multiply_add_fusion
  235.2 1.6 multiply_reduce_fusion.1
  236.8 74.2 %psum.23 = f32[]{:T(128)} all-reduce(f32[]{:T(128)} %get-tuple-element.7), channel_id=1, replica_groups=mesh['ax'=64,'sec'=4] {'ax','sec'}, use_global_device_ids=true, to_apply=%region_7.8 | all-reduce | flops 1 | bytes 8 | tf_op jit(solution)/shard_map/psum | solution.py:89
  (40 shorter events, 1.5 us)
Async XLA Ops:
  7.2 17.8 %copy-start = (f32[6,6,1024]{2,1,0:T(8,128)S(1)}, f32[6,6,1024]{2,1,0:T(8,128)}, u32[]{:S(2)}) copy-start(f32[6,6,1024]{2,1,0:T(8,128)} %param.13) | copy-start | bytes 442372
  7.2 14.6 %copy-start.1 = (f32[128,6,256]{2,0,1:T(8,128)S(1)}, f32[128,6,256]{2,0,1:T(8,128)}, u32[]{:S(2)}) copy-start(f32[128,6,256]{2,0,1:T(8,128)} %param.8) | copy-start | bytes 2359300
  7.2 15.9 %copy-start.9 = (f32[128,6,256]{2,0,1:T(8,128)S(1)}, f32[128,6,256]{2,0,1:T(8,128)}, u32[]{:S(2)}) copy-start(f32[128,6,256]{2,0,1:T(8,128)} %param.7) | copy-start | bytes 2359300
  7.2 15.9 %copy-start.6 = (f32[128,6,256]{2,0,1:T(8,128)S(1)}, f32[128,6,256]{2,0,1:T(8,128)}, u32[]{:S(2)}) copy-start(f32[128,6,256]{2,0,1:T(8,128)} %param.9) | copy-start | bytes 2359300
  7.2 56.9 %all-gather.2.cloned.1.call-start = ((), (), s32[]{:S(2)}) async-start(), calls=%async_computation.1 | async-start | bytes 3932160 | tf_op jit(solution)/shard_map/all_gather | solution.py:65
  9.5 12.4 %collective-permute-start.2 = (f32[128,6,1]{2,0,1:T(8,128)}, f32[128,6,1]{2,0,1:T(8,128)S(1)}, u32[]{:S(2)}, u32[]{:S(2)}) collective-permute-start(f32[128,6,1]{2,0,1:T(8,128)} %get-tuple-element.16), channel_id=1, source_target_pairs={{1,0},{2,1},{3,2},{0,3},{5,4},{6,5},{7,6},{4,7},{9,8},{10,9},{11,1... | collective-permute-start | bytes 9224 | tf_op jit(solution)/shard_map/ppermute | solution.py:16
  12.8 10.3 %collective-permute-start.3 = (f32[128,6,1]{2,0,1:T(8,128)}, f32[128,6,1]{2,0,1:T(8,128)S(1)}, u32[]{:S(2)}, u32[]{:S(2)}) collective-permute-start(f32[128,6,1]{2,0,1:T(8,128)} %get-tuple-element.17), channel_id=1, source_target_pairs={{0,1},{1,2},{2,3},{3,0},{4,5},{5,6},{6,7},{7,4},{8,9},{9,10},{10,1... | collective-permute-start | bytes 9224 | tf_op jit(solution)/shard_map/ppermute | solution.py:15
  14.7 8.4 %collective-permute-start = (f32[1,6,256]{2,0,1:T(1,128)S(1)}, f32[1,6,256]{2,0,1:T(1,128)S(1)}, u32[]{:S(2)}, u32[]{:S(2)}) collective-permute-start(f32[1,6,256]{2,0,1:T(1,128)S(1)} %get-tuple-element.14), channel_id=1, source_target_pairs={{4,0},{8,4},{12,8},{16,12},{20,16},{24,20},{28,24},{32,28},{36,32}... | collective-permute-start | bytes 18440 | tf_op jit(solution)/shard_map/ppermute | solution.py:16
  16.0 7.1 %collective-permute-start.1 = (f32[1,6,256]{2,0,1:T(1,128)S(1)}, f32[1,6,256]{2,0,1:T(1,128)S(1)}, u32[]{:S(2)}, u32[]{:S(2)}) collective-permute-start(f32[1,6,256]{2,0,1:T(1,128)S(1)} %get-tuple-element.15), channel_id=1, source_target_pairs={{0,4},{4,8},{8,12},{12,16},{16,20},{20,24},{24,28},{28,32},{32,36}... | collective-permute-start | bytes 18440 | tf_op jit(solution)/shard_map/ppermute | solution.py:15
  24.7 109.5 %reduce-scatter.2.cloned.1.call-start = ((), (), s32[]{:S(2)}) async-start(), calls=%async_computation.2 | async-start | bytes 3932160 | tf_op jit(solution)/shard_map/reduce_scatter | solution.py:72
  135.5 1.4 copy-start.5
  135.9 1.1 copy-start.3
  137.0 15.8 %copy-start.2 = (f32[128,6,256]{2,0,1:T(8,128)S(1)}, f32[128,6,256]{2,0,1:T(8,128)}, u32[]{:S(2)}) copy-start(f32[128,6,256]{2,0,1:T(8,128)} %fusion.18) | copy-start | bytes 2359300
  139.6 13.2 %copy-start.4 = (f32[128,6,256]{2,0,1:T(8,128)S(1)}, f32[128,6,256]{2,0,1:T(8,128)}, u32[]{:S(2)}) copy-start(f32[128,6,256]{2,0,1:T(8,128)} %copy-done.3) | copy-start | bytes 2359300
  139.6 13.2 %copy-start.7 = (f32[128,6,256]{2,0,1:T(8,128)S(1)}, f32[128,6,256]{2,0,1:T(8,128)}, u32[]{:S(2)}) copy-start(f32[128,6,256]{2,0,1:T(8,128)} %param.9) | copy-start | bytes 2359300
  139.6 13.2 %collective-permute-start.6 = (f32[128,6,1]{2,0,1:T(8,128)}, f32[128,6,1]{2,0,1:T(8,128)S(1)}, u32[]{:S(2)}, u32[]{:S(2)}) collective-permute-start(f32[128,6,1]{2,0,1:T(8,128)} %get-tuple-element.12), channel_id=1, source_target_pairs={{1,0},{2,1},{3,2},{0,3},{5,4},{6,5},{7,6},{4,7},{9,8},{10,9},{11,1... | collective-permute-start | bytes 9224 | tf_op jit(solution)/shard_map/ppermute | solution.py:16
  140.3 12.5 %collective-permute-start.7 = (f32[128,6,1]{2,0,1:T(8,128)S(1)}, f32[128,6,1]{2,0,1:T(8,128)S(1)}, u32[]{:S(2)}, u32[]{:S(2)}) collective-permute-start(f32[128,6,1]{2,0,1:T(8,128)S(1)} %get-tuple-element.13), channel_id=1, source_target_pairs={{0,1},{1,2},{2,3},{3,0},{4,5},{5,6},{6,7},{7,4},{8,9},{9,10},{10,1... | collective-permute-start | bytes 9224 | tf_op jit(solution)/shard_map/ppermute | solution.py:15
  142.8 9.9 %collective-permute-start.4 = (f32[1,6,256]{2,0,1:T(1,128)S(1)}, f32[1,6,256]{2,0,1:T(1,128)S(1)}, u32[]{:S(2)}, u32[]{:S(2)}) collective-permute-start(f32[1,6,256]{2,0,1:T(1,128)S(1)} %get-tuple-element.10), channel_id=1, source_target_pairs={{4,0},{8,4},{12,8},{16,12},{20,16},{24,20},{28,24},{32,28},{36,32}... | collective-permute-start | bytes 18440 | tf_op jit(solution)/shard_map/ppermute | solution.py:16
  144.1 8.6 %collective-permute-start.5 = (f32[1,6,256]{2,0,1:T(1,128)S(1)}, f32[1,6,256]{2,0,1:T(1,128)S(1)}, u32[]{:S(2)}, u32[]{:S(2)}) collective-permute-start(f32[1,6,256]{2,0,1:T(1,128)S(1)} %get-tuple-element.11), channel_id=1, source_target_pairs={{0,4},{4,8},{8,12},{12,16},{16,20},{20,24},{24,28},{28,32},{32,36}... | collective-permute-start | bytes 18440 | tf_op jit(solution)/shard_map/ppermute | solution.py:15
  234.0 1.2 copy-start.8
Sparse Core Ops, SparseCore 0:
  24.8 39.2 all-gather.1
  85.0 49.0 reduce-scatter.1
where the time goes:
time: 320 us; the launch traced here: 319 us
  blocking collectives  152 us (48%)
  waiting for transfers between devices  88.8 us (28%)
  starting transfers between devices  18.4 us (6%)
  between operations  16.3 us (5%)
  matrix products  16.1 us (5%)
  other arithmetic  14.5 us (5%)
  local copies, waits for them, and re-layouts  13.1 us (4%)
    psum x1, blocking collectives, shards(): inner_rz = lax.psum(jnp.sum(residual * prec), ('ax', 'sec')) / cell_total  77.7 us
    psum x1, blocking collectives, shards(): lax.psum(jnp.sum(residual_new * residual_new), ('ax', 'sec')) / cell_total  74.2 us
    reduce_scatter x1, waiting for transfers between devices, shards(): lax.psum_scatter(lax.dot_general(table_rows, scaled, (((1,), (1,)), ((),...  49.2 us
    all_gather x1, waiting for transfers between devices, shards(): piece = lax.all_gather(residual, 'sec', axis=2, tiled=True)  35.1 us
    ppermute x4, starting transfers between devices, with_halo(): before = lax.ppermute(last, axis, up)  11.6 us
    dot_general x1, matrix products, shards(): lax.dot_general(table_rows, scaled, (((1,), (1,)), ((), ())), precision=l...  8.26 us
    dot_general x1, matrix products, shards(): jnp.dot(flat, table_rows, precision=lax.Precision.HIGHEST)  6.95 us
    ppermute x4, starting transfers between devices, with_halo(): after = lax.ppermute(first, axis, down)  6.5 us
  transfers between devices with their start and end apart: 10, of which 4 were waited for; matrix products, arithmetic and copies ran while one was open for 3% of the time, Pallas kernels for 0%

commit v1 on v0

--- a/solution.py
+++ b/solution.py
@@ -62,7 +62,9 @@
     table = harmonic_table(jnp.arange(around_cells), own_index, around_cells)
     own_inverse = lax.dynamic_slice_in_dim(precond, sector * sector_width, sector_width, 2)
     initial = jnp.zeros((slab_count, comp_count, 2 * sector_width), jnp.float32)
-    piece = lax.all_gather(residual, "sec", axis=2, tiled=True)
+    piece = jnp.concatenate(
+        lax.all_to_all(jnp.stack([residual] * lax.axis_size("sec")), "sec", 0, 0), axis=2
+    )
     span = piece.shape[2]
     table_rows = table
     flat = piece.reshape(-1, span)

time: 320 us -> 331 us (1.034)
  local copies, waits for them, and re-layouts: 13.1 us -> 20 us
  starting transfers between devices: 18.4 us -> 24.6 us
    all_gather x1 -> x0, waiting for transfers between devices: 35.1 us -> none  [shards(): piece = lax.all_gather(residual, 'sec', axis=2, tiled=True)]
    all_to_all x0 -> x1, waiting for transfers between devices: none -> 32.3 us  [shards(): lax.all_to_all(jnp.stack([residual] * lax.axis_size('sec')), 'sec', 0, 0)]
    all_to_all x0 -> x1, starting transfers between devices: none -> 6.45 us  [shards(): lax.all_to_all(jnp.stack([residual] * lax.axis_size('sec')), 'sec', 0, 0)]
    another operation x0 -> x2, local copies, waits for them, and re-layouts: none -> 4.47 us
where the time goes in v1:
time: 331 us
  blocking collectives  152 us (46%)
  waiting for transfers between devices  87.9 us (27%)
  starting transfers between devices  24.6 us (7%)
  local copies, waits for them, and re-layouts  20 us (6%)
  between operations  16.3 us (5%)
  other arithmetic  15.9 us (5%)
  matrix products  14.3 us (4%)
    psum x1, blocking collectives, shards(): inner_rz = lax.psum(jnp.sum(residual * prec), ('ax', 'sec')) / cell_total  77.5 us
    psum x1, blocking collectives, shards(): lax.psum(jnp.sum(residual_new * residual_new), ('ax', 'sec')) / cell_total  74.2 us
    reduce_scatter x1, waiting for transfers between devices, shards(): lax.psum_scatter(lax.dot_general(table_rows, scaled, (((1,), (1,)), ((),...  51.6 us
    all_to_all x1, waiting for transfers between devices, shards(): lax.all_to_all(jnp.stack([residual] * lax.axis_size('sec')), 'sec', 0, 0)  32.3 us
    ppermute x4, starting transfers between devices, with_halo(): before = lax.ppermute(last, axis, up)  11.6 us
    dot_general x1, matrix products, shards(): lax.dot_general(table_rows, scaled, (((1,), (1,)), ((), ())), precision=l...  8.18 us
  transfers between devices with their start and end apart: 10, of which 4 were waited for; matrix products, arithmetic and copies ran while one was open for 3% of the time, Pallas kernels for 0%

profile of v1, /device:TPU:1, one launch (start us, length us, event | category | flops | bytes accessed | tf_op | source)
XLA Modules:
  0.0 330.6 jit_solution(6690771843932140278)
XLA Ops:
  7.2 2.1 fusion.30
  9.2 3.2 collective-permute-start.2
  12.5 1.1 collective-permute-start.3
  14.4 1.3 collective-permute-start
  15.7 4.0 %collective-permute-start.1 = (f32[1,6,256]{2,0,1:T(1,128)S(1)}, f32[1,6,256]{2,0,1:T(1,128)S(1)}, u32[]{:S(2)}, u32[]{:S(2)}) collective-permute-start(f32[1,6,256]{2,0,1:T(1,128)S(1)} %get-tuple-element.18), channel_id=1, source_target_pairs={{0,4},{4,8},{8,12},{12,16},{16,20},{20,24},{24,28},{28,32},{32,36}... | collective-permute-start | bytes 18440 | tf_op jit(solution)/shard_map/ppermute | solution.py:15
  19.7 0.9 subtract_convert_fusion
  20.7 1.0 convolution_multiply_fusion.1
  23.0 1.7 fusion.18
  24.7 2.0 stack.19
  26.7 6.5 %all-to-all-start = ((f32[4,128,6,256]{3,1,2,0:T(8,128)}), f32[4,128,6,256]{3,1,2,0:T(8,128)}, u32[]{:S(2)}, u32[]{:S(2)}) async-start(f32[4,128,6,256]{3,1,2,0:T(8,128)} %stack.19), calls=%async_computation | async-start | bytes 6291456 | tf_op jit(solution)/shard_map/all_to_all | solution.py:66
  33.2 5.4 %fusion.22 = (f32[1024,256]{1,0:T(8,128)S(1)}, f32[1024,256]{1,0:T(8,128)}) fusion(s32[256]{0:T(256)S(1)} %iota_add_fusion), kind=kLoop, calls=%fused_computation.47 | loop fusion | flops 3670016 | bytes 2098176 | tf_op jit(solution)/shard_map/cos | solution.py:38
  38.6 32.3 %all-to-all-done = f32[4,128,6,256]{3,1,2,0:T(8,128)} async-done(((f32[4,128,6,256]{3,1,2,0:T(8,128)}), f32[4,128,6,256]{3,1,2,0:T(8,128)}, u32[]{:S(2)}, u32[]{:S(2)}) %all-to-all-start) | async-done | bytes 3145760 | tf_op jit(solution)/shard_map/all_to_all | solution.py:66
  70.9 2.4 copy.53
  73.3 5.1 %fusion = f32[128,6,512]{2,0,1:T(8,128)S(1)} fusion(f32[128,6,1024]{2,0,1:T(8,128)S(1)} %bitcast.20, f32[1024,256]{1,0:T(8,128)S(1)} %copy-done.2, f32[1024,256]{1,0:T(8,128)S(1)} %get-tuple-element.21), kind=kOutput, calls=%fused_computation.2 | convolution fusion | flops 4832362496 | bytes 6815744 | tf_op jit(solution)/shard_map/dot_general | solution.py:71
  79.1 2.3 copy.48
  81.4 2.6 reshape.56
  84.0 8.2 %convolution_multiply_fusion = f32[1024,768]{1,0:T(8,128)} fusion(f32[768,512]{1,0:T(8,128)} %reshape.56, f32[1024,256]{1,0:T(8,128)} %get-tuple-element.22, f32[1024,256]{1,0:T(8,128)S(1)} %get-tuple-element.21), kind=kOutput, calls=%fused_computation.4 | convolution fusion | flops 4833148928 | bytes 6815744 | tf_op jit(solution)/shard_map/dot_general | solution.py:75
  92.2 51.6 %reduce-scatter.2.cloned.1.call-done = f32[256,768]{1,0:T(8,128)} async-done(((f32[1024,768]{1,0:T(8,128)}), f32[256,768]{1,0:T(8,128)}) %reduce-scatter.2.cloned.1.call-update) | async-done | bytes 786448 | tf_op jit(solution)/shard_map/reduce_scatter | solution.py:74
  143.8 2.3 copy.49
  146.1 1.2 reshape.57
  147.6 1.0 fusion.28
  148.6 2.5 reshape.58
  151.8 2.6 collective-permute-start.7
  154.4 1.3 collective-permute-start.4
  155.6 4.0 %collective-permute-start.5 = (f32[1,6,256]{2,0,1:T(1,128)S(1)}, f32[1,6,256]{2,0,1:T(1,128)S(1)}, u32[]{:S(2)}, u32[]{:S(2)}) collective-permute-start(f32[1,6,256]{2,0,1:T(1,128)S(1)} %get-tuple-element.14), channel_id=1, source_target_pairs={{0,4},{4,8},{8,12},{12,16},{16,20},{20,24},{24,28},{28,32},{32,36}... | collective-permute-start | bytes 18440 | tf_op jit(solution)/shard_map/ppermute | solution.py:15
  159.6 1.2 copy_multiply_fusion
  160.9 3.5 %collective-permute-done.6 = f32[128,6,1]{2,0,1:T(8,128)S(1)} collective-permute-done((f32[128,6,1]{2,0,1:T(8,128)}, f32[128,6,1]{2,0,1:T(8,128)S(1)}, u32[]{:S(2)}, u32[]{:S(2)}) %collective-permute-start.6) | collective-permute-done | bytes 3104 | tf_op jit(solution)/shard_map/ppermute | solution.py:16
  164.5 2.2 multiply_reduce_fusion.2
  166.6 77.5 %all-reduce = (f32[]{:T(128)}, f32[]{:T(128)}) all-reduce(f32[]{:T(128)} %get-tuple-element.7, f32[]{:T(128)} %get-tuple-element.6), channel_id=1, replica_groups=mesh['ax'=64,'sec'=4] {'ax','sec'}, use_global_device_ids=true, to_apply=%region_3.4 | all-reduce | flops 2 | bytes 16 | tf_op jit(solution)/shard_map/psum | solution.py:87
  245.5 1.2 multiply_add_fusion
  246.7 1.6 multiply_reduce_fusion.1
  248.3 74.2 %psum.23 = f32[]{:T(128)} all-reduce(f32[]{:T(128)} %get-tuple-element.10), channel_id=1, replica_groups=mesh['ax'=64,'sec'=4] {'ax','sec'}, use_global_device_ids=true, to_apply=%region_7.8 | all-reduce | flops 1 | bytes 8 | tf_op jit(solution)/shard_map/psum | solution.py:91
  (41 shorter events, 4.6 us)
Async XLA Ops:
  7.2 26.0 %copy-start = (f32[6,6,1024]{2,1,0:T(8,128)S(1)}, f32[6,6,1024]{2,1,0:T(8,128)}, u32[]{:S(2)}) copy-start(f32[6,6,1024]{2,1,0:T(8,128)} %param.13) | copy-start | bytes 442372
  7.2 14.5 %copy-start.1 = (f32[128,6,256]{2,0,1:T(8,128)S(1)}, f32[128,6,256]{2,0,1:T(8,128)}, u32[]{:S(2)}) copy-start(f32[128,6,256]{2,0,1:T(8,128)} %param.8) | copy-start | bytes 2359300
  9.2 12.6 %collective-permute-start.2 = (f32[128,6,1]{2,0,1:T(8,128)}, f32[128,6,1]{2,0,1:T(8,128)S(1)}, u32[]{:S(2)}, u32[]{:S(2)}) collective-permute-start(f32[128,6,1]{2,0,1:T(8,128)} %get-tuple-element.19), channel_id=1, source_target_pairs={{1,0},{2,1},{3,2},{0,3},{5,4},{6,5},{7,6},{4,7},{9,8},{10,9},{11,1... | collective-permute-start | bytes 9224 | tf_op jit(solution)/shard_map/ppermute | solution.py:16
  12.5 9.8 %collective-permute-start.3 = (f32[128,6,1]{2,0,1:T(8,128)S(1)}, f32[128,6,1]{2,0,1:T(8,128)S(1)}, u32[]{:S(2)}, u32[]{:S(2)}) collective-permute-start(f32[128,6,1]{2,0,1:T(8,128)S(1)} %get-tuple-element.20), channel_id=1, source_target_pairs={{0,1},{1,2},{2,3},{3,0},{4,5},{5,6},{6,7},{7,4},{8,9},{9,10},{10,1... | collective-permute-start | bytes 9224 | tf_op jit(solution)/shard_map/ppermute | solution.py:15
  14.4 7.9 %collective-permute-start = (f32[1,6,256]{2,0,1:T(1,128)S(1)}, f32[1,6,256]{2,0,1:T(1,128)S(1)}, u32[]{:S(2)}, u32[]{:S(2)}) collective-permute-start(f32[1,6,256]{2,0,1:T(1,128)S(1)} %get-tuple-element.17), channel_id=1, source_target_pairs={{4,0},{8,4},{12,8},{16,12},{20,16},{24,20},{28,24},{32,28},{36,32}... | collective-permute-start | bytes 18440 | tf_op jit(solution)/shard_map/ppermute | solution.py:16
  15.7 7.3 %collective-permute-start.1 = (f32[1,6,256]{2,0,1:T(1,128)S(1)}, f32[1,6,256]{2,0,1:T(1,128)S(1)}, u32[]{:S(2)}, u32[]{:S(2)}) collective-permute-start(f32[1,6,256]{2,0,1:T(1,128)S(1)} %get-tuple-element.18), channel_id=1, source_target_pairs={{0,4},{4,8},{8,12},{12,16},{16,20},{20,24},{24,28},{28,32},{32,36}... | collective-permute-start | bytes 18440 | tf_op jit(solution)/shard_map/ppermute | solution.py:15
  20.6 2.4 copy-start.5
  20.7 2.4 copy-start.8
  22.3 0.7 copy-start.9
  26.7 44.1 %all-to-all-start = ((f32[4,128,6,256]{3,1,2,0:T(8,128)}), f32[4,128,6,256]{3,1,2,0:T(8,128)}, u32[]{:S(2)}, u32[]{:S(2)}) async-start(f32[4,128,6,256]{3,1,2,0:T(8,128)} %stack.19), calls=%async_computation | async-start | bytes 6291456 | tf_op jit(solution)/shard_map/all_to_all | solution.py:66
  33.2 110.6 %reduce-scatter.2.cloned.1.call-start = ((), (), s32[]{:S(2)}) async-start(), calls=%async_computation.2 | async-start | bytes 3932160 | tf_op jit(solution)/shard_map/reduce_scatter | solution.py:74
  70.9 2.5 copy-start.2
  147.6 1.0 copy-start.3
  151.1 13.4 %copy-start.4 = (f32[128,6,256]{2,0,1:T(8,128)S(1)}, f32[128,6,256]{2,0,1:T(8,128)}, u32[]{:S(2)}) copy-start(f32[128,6,256]{2,0,1:T(8,128)} %copy-done.3) | copy-start | bytes 2359300
  151.1 13.4 %copy-start.6 = (f32[128,6,256]{2,0,1:T(8,128)S(1)}, f32[128,6,256]{2,0,1:T(8,128)}, u32[]{:S(2)}) copy-start(f32[128,6,256]{2,0,1:T(8,128)} %param.9) | copy-start | bytes 2359300
  151.1 13.3 %collective-permute-start.6 = (f32[128,6,1]{2,0,1:T(8,128)}, f32[128,6,1]{2,0,1:T(8,128)S(1)}, u32[]{:S(2)}, u32[]{:S(2)}) collective-permute-start(f32[128,6,1]{2,0,1:T(8,128)} %get-tuple-element.15), channel_id=1, source_target_pairs={{1,0},{2,1},{3,2},{0,3},{5,4},{6,5},{7,6},{4,7},{9,8},{10,9},{11,1... | collective-permute-start | bytes 9224 | tf_op jit(solution)/shard_map/ppermute | solution.py:16
  151.8 12.7 %collective-permute-start.7 = (f32[128,6,1]{2,0,1:T(8,128)S(1)}, f32[128,6,1]{2,0,1:T(8,128)S(1)}, u32[]{:S(2)}, u32[]{:S(2)}) collective-permute-start(f32[128,6,1]{2,0,1:T(8,128)S(1)} %get-tuple-element.16), channel_id=1, source_target_pairs={{0,1},{1,2},{2,3},{3,0},{4,5},{5,6},{6,7},{7,4},{8,9},{9,10},{10,1... | collective-permute-start | bytes 9224 | tf_op jit(solution)/shard_map/ppermute | solution.py:15
  154.4 10.1 %collective-permute-start.4 = (f32[1,6,256]{2,0,1:T(1,128)S(1)}, f32[1,6,256]{2,0,1:T(1,128)S(1)}, u32[]{:S(2)}, u32[]{:S(2)}) collective-permute-start(f32[1,6,256]{2,0,1:T(1,128)S(1)} %get-tuple-element.13), channel_id=1, source_target_pairs={{4,0},{8,4},{12,8},{16,12},{20,16},{24,20},{28,24},{32,28},{36,32}... | collective-permute-start | bytes 18440 | tf_op jit(solution)/shard_map/ppermute | solution.py:16
  155.6 8.8 %collective-permute-start.5 = (f32[1,6,256]{2,0,1:T(1,128)S(1)}, f32[1,6,256]{2,0,1:T(1,128)S(1)}, u32[]{:S(2)}, u32[]{:S(2)}) collective-permute-start(f32[1,6,256]{2,0,1:T(1,128)S(1)} %get-tuple-element.14), channel_id=1, source_target_pairs={{0,4},{4,8},{8,12},{12,16},{16,20},{20,24},{24,28},{28,32},{32,36}... | collective-permute-start | bytes 18440 | tf_op jit(solution)/shard_map/ppermute | solution.py:15
  245.5 1.2 copy-start.7
Sparse Core Ops, SparseCore 0:
  92.3 51.4 reduce-scatter.1
